TPU v7x, 32 devices: a whole 2x2x4 slice. The times are simulated.
32 devices in a mesh: aa: 8 (over y, x, core), ba: 4 (over z).
Axes of the slice: x: 2, y: 2, z: 4, core: 2. Of those that a mesh axis runs over, the one named last changes fastest.
Arguments:
- amplitudes: bfloat16 [1024, 2048], P('ba', 'aa'), may hold values from -6 to 6
- integrals: bfloat16 [512, 512, 2048], P('aa', 'ba'), may hold values from -0.125 to 0.125
- virt_energy: float32 [512], replicated, may hold values from 0.2 to 2
- pair_energy: float32 [1024], replicated, may hold values from 0.3 to 3
Outputs:
- update: float32 [512, 512, 1024], P('aa', 'ba')
All inputs are finite; a program needn't handle non-finite values.
Results may differ from a plain program's by a relative error of at most 0.0003.
Values may be sent and summed in bfloat16 or wider, within the bound.
A program may use at most 128 MiB of HBM per device.

v0:
```python
import jax
import jax.numpy as jnp
from jax import lax
from jax.sharding import PartitionSpec as P


def contract(left, right):
    return lax.dot_general(
        left, right, (((1,), (1,)), ((), ())), preferred_element_type=jnp.float32
    )


def on_device(amplitudes, integrals, virt_energy, pair_energy):
    first_count = integrals.shape[0]
    second_count = integrals.shape[1]
    cd_count = integrals.shape[2]
    flat_ints = integrals.reshape(first_count * second_count, cd_count)
    all_rows = lax.all_gather(amplitudes, "ba", axis=0, tiled=True)
    whole = lax.all_gather(all_rows, "aa", axis=1, tiled=True)
    ladder = contract(flat_ints, whole)
    pair_total = ladder.shape[1]
    ladder = ladder.reshape(first_count, second_count, pair_total)
    first_energy = lax.dynamic_slice_in_dim(
        virt_energy, lax.axis_index("aa") * first_count, first_count, 0
    )
    second_energy = lax.dynamic_slice_in_dim(
        virt_energy, lax.axis_index("ba") * second_count, second_count, 0
    )
    denom = first_energy[:, None, None] + second_energy[None, :, None] + pair_energy[None, None, :]
    return ladder / denom


def solution(mesh):
    placed = (P("ba", "aa"), P("aa", "ba", None), P(), P())
    return jax.shard_map(
        on_device, mesh=mesh, in_specs=placed, out_specs=P("aa", "ba", None), check_vma=False
    )
```

profile of v0, /device:TPU:0, one launch (start us, length us, event | category | flops | bytes accessed | tf_op | source)
XLA Modules:
  0.0 112.0 jit_solution(7729294179379284813)
XLA Ops:
  6.5 0.0 all-gather.2.cloned.1.call-start
  6.5 19.4 %all_gather.6 = bf16[1024,256]{1,0:T(8,128)(2,1)} all-gather(bf16[256,256]{1,0:T(8,128)(2,1)} %param.4), channel_id=1, replica_groups=mesh['aa'=8,'ba'=4] {'ba'}, dimensions={0}, use_global_device_ids=true | all-gather | bytes 655360 | tf_op jit(solution)/shard_map/all_gather | solution.py:18
  25.9 0.0 all-gather.2.cloned.1.call-update
  25.9 0.8 dynamic_slice.7
  26.7 0.8 dynamic_slice.6
  27.4 0.1 broadcast_add_fusion
  27.5 35.6 %all-gather.2.cloned.1.call-done = bf16[1024,2048]{1,0:T(8,128)(2,1)} async-done(((bf16[1024,256]{1,0:T(8,128)(2,1)}), bf16[1024,2048]{1,0:T(8,128)(2,1)}) %all-gather.2.cloned.1.call-update) | async-done | bytes 4194320 | tf_op jit(solution)/shard_map/all_gather | solution.py:19
  63.1 42.0 %add_divide_fusion = f32[64,128,1024]{2,1,0:T(8,128)} fusion(f32[1024]{0:T(1024)} %param.7, f32[64,128]{1,0:T(8,128)S(1)} %broadcast_add_fusion, bf16[64,128,2048]{2,1,0:T(8,128)(2,1)} %param.5, bf16[1024,2048]{1,0:T(8,128)(2,1)} %all-gather.2.cloned.1.call-done), kind=kOutput, calls=%fused_computation | convolution fusion | flops 34376515584 | bytes 71340032 | tf_op jit(solution)/shard_map/dot_general | solution.py:8
Async XLA Ops:
  6.5 56.6 %all-gather.2.cloned.1.call-start = ((), (), s32[]{:S(2)}) async-start(), calls=%async_computation | async-start | bytes 4718592 | tf_op jit(solution)/shard_map/all_gather | solution.py:19
Sparse Core Ops, SparseCore 0:
  26.0 37.0 all-gather.1
where the time goes:
time: 112 us
  matrix products  42 us (38%)
  waiting for transfers between devices  35.6 us (32%)
  blocking collectives  19.4 us (17%)
  between operations  13.4 us (12%)
  local copies, waits for them, and re-layouts  1.51 us (1%)
    dot_general x1, matrix products, contract(): lax.dot_general(left, right, (((1,), (1,)), ((), ())), preferred_element_...  42 us
    all_gather x1, waiting for transfers between devices, on_device(): whole = lax.all_gather(all_rows, 'aa', axis=1, tiled=True)  35.6 us
    all_gather x1, blocking collectives, on_device(): all_rows = lax.all_gather(amplitudes, 'ba', axis=0, tiled=True)  19.4 us
  transfers between devices with their start and end apart: 1, of which 1 were waited for; matrix products, arithmetic and copies ran while one was open for 1% of the time, Pallas kernels for 0%

commit v1 on v0

v1 whole, which is shorter than its diff:
```python
import functools

import jax
import jax.numpy as jnp
from jax import lax
from jax.experimental import pallas as pl
from jax.experimental.pallas import tpu as pltpu
from jax.sharding import PartitionSpec as P

MESH = pl.DeviceIdType.MESH
CORES, SIDE = 2, 2
EARLY, SEGMENTS = 3, 8
GROUP, COLUMNS = 8, 2


def contract(left, right):
    return lax.dot_general(
        left, right, (((1,), (1,)), ((), ())), preferred_element_type=jnp.float32
    )


def pick(index, options):
    total = jnp.int32(0)
    for value, option in enumerate(options):
        total = total + jnp.where(index == value, jnp.int32(option), jnp.int32(0))
    return total


def gather_kernel(nb, early_rows, amp_ref, ints_ref, whole_ref, part_ref,
                  whole, ints, acc, recv_sem, send_sem, part_sem, load_sem, out_sem):
    a, b = lax.axis_index("aa"), lax.axis_index("ba")
    rows, cols = amp_ref.shape
    wide = CORES * cols
    groups, group_rows = ints_ref.shape[0], ints_ref.shape[1]
    late_rows = group_rows - early_rows
    core, chip = a % CORES, a // CORES
    x, y = chip % SIDE, chip // SIDE
    chips = [chip, y * SIDE + (1 - x), (1 - y) * SIDE + x, (1 - y) * SIDE + (1 - x)]
    partner = chip * CORES + (1 - core)
    x_dev, y_dev = chips[1] * CORES + core, chips[2] * CORES + core
    tables = [sorted(range(nb), key=lambda v: (abs(v - own), v)) for own in range(nb)]
    order = [b] + [pick(b, [tables[own][k] for own in range(nb)]) for k in range(1, nb)]
    up, down = b + 1, b - 1

    def load(q):
        span = pl.ds(pl.multiple_of(chips[q] * wide, wide), wide)
        return pltpu.make_async_copy(
            ints_ref.at[:, pl.ds(late_rows, early_rows), span], ints.at[q], load_sem.at[q]
        )

    for q in range(4):
        load(q).start()

    barrier = pltpu.get_barrier_semaphore()
    for dev in (partner, x_dev, y_dev):
        pl.semaphore_signal(barrier, inc=1, device_id=(dev, b), device_id_type=MESH)

    @pl.when(up < nb)
    def _():
        pl.semaphore_signal(barrier, inc=1, device_id=(a, up), device_id_type=MESH)

    @pl.when(down >= 0)
    def _():
        pl.semaphore_signal(barrier, inc=1, device_id=(a, down), device_id_type=MESH)

    peers = 3 + jnp.where(up < nb, 1, 0) + jnp.where(down >= 0, 1, 0)
    pl.semaphore_wait(barrier, peers)

    def slot(q, c, k):
        row = pl.ds(pl.multiple_of(order[k] * rows, rows), rows)
        col = pl.ds(pl.multiple_of(chips[q] * wide + c * cols, cols), cols)
        return whole.at[row, col]

    def remote(q, k, kind, dev, src=None):
        place = slot(q, core, k)
        sem = recv_sem.at[(chips[q] * CORES + core) * nb + order[k]]
        return pltpu.make_async_remote_copy(
            src_ref=place if src is None else src, dst_ref=place,
            send_sem=send_sem.at[kind * nb + k], recv_sem=sem,
            device_id=dev, device_id_type=MESH,
        )

    def arrived(q, c, k):
        place = slot(q, c, k)
        sem = recv_sem.at[(chips[q] * CORES + c) * nb + order[k]]
        pltpu.make_async_copy(place, place, sem).wait()

    def along(k):
        if k == 0:
            return [(0, up < nb, (a, up)), (9, down >= 0, (a, down))]
        below = order[k] < b
        return [(0, below & (up < nb), (a, up)), (9, (order[k] > b) & (down >= 0), (a, down))]

    def sends(q, k):
        found = [(1 + q, (partner, b))]
        if q == 0:
            found += [(5, (x_dev, b)), (6, (y_dev, b))]
        if q == 1 and k % 2 == 0:
            found += [(7, (y_dev, b))]
        if q == 2 and k % 2 == 1:
            found += [(8, (x_dev, b))]
        return found

    def forward(q, k, src=None):
        if q == 0:
            for kind, cond, dev in along(k):
                @pl.when(cond)
                def _():
                    remote(q, k, kind, dev, src).start()
            for kind, dev in reversed(sends(q, k)):
                remote(q, k, kind, dev, src).start()
        else:
            for kind, dev in reversed(sends(q, k)):
                remote(q, k, kind, dev, src).start()

    def multiply(q, k, first):
        row = pl.ds(pl.multiple_of(order[k] * rows, rows), rows)
        col = pl.ds(pl.multiple_of(chips[q] * wide, wide), wide)
        right = whole[row, col]

        def body(g, carry):
            left = ints[q, pl.ds(g * GROUP, GROUP)].reshape(GROUP * early_rows, wide)
            value = contract(left, right)
            place = pl.ds(g * GROUP * early_rows, GROUP * early_rows)
            acc[k, place] = value if first else acc[k, place] + value
            return carry

        lax.fori_loop(0, groups // GROUP, body, 0)

    forward(0, 0, amp_ref)
    mine = pltpu.make_async_copy(amp_ref, slot(0, core, 0), part_sem.at[0])
    mine.start()
    mine.wait()

    stages = [[(0, 0)]]
    for s in range(1, nb + 3):
        stage = [(0, s)] if s < nb else []
        if s - 1 < nb:
            stage += [(1, s - 1), (2, s - 1)]
        if 2 <= s and s - 2 < nb:
            stage += [(3, s - 2)]
        stages.append(stage)
    loaded, done = set(), {k: 0 for k in range(nb)}

    def partner_ready(stage):
        for q, k in stage:
            arrived(q, 1 - core, k)

    def product(q, k):
        if q not in loaded:
            load(q).wait()
            loaded.add(q)
        multiply(q, k, done[k] == 0)
        done[k] += 1
        if done[k] == 4:
            out_copy(k).start()

    def out_copy(k):
        col = pl.ds(pl.multiple_of(order[k] * rows, rows), rows)
        return pltpu.make_async_copy(acc.at[k], part_ref.at[:, col], out_sem.at[k])

    def whole_copy(k):
        row = pl.ds(pl.multiple_of(order[k] * rows, rows), rows)
        return pltpu.make_async_copy(whole.at[row], whole_ref.at[row], part_sem.at[1 + k])

    flat = []
    for s in range(len(stages) + 1):
        now = stages[s] if s < len(stages) else []
        before = stages[s - 1] if s > 0 else []
        if s > 0:
            for q, k in now:
                arrived(q, core, k)
                forward(q, k)
        for q, k in before:
            arrived(q, 1 - core, k)
        for q, k in before:
            product(q, k)
        for q, k in before:
            if q == 3:
                whole_copy(k).start()

    for k in range(nb):
        for kind, cond, dev in along(k):
            @pl.when(cond)
            def _():
                remote(0, k, kind, dev).wait_send()
        for q in range(4):
            for kind, dev in sends(q, k):
                remote(q, k, kind, dev).wait_send()
    for k in range(nb):
        whole_copy(k).wait()
        out_copy(k).wait()


def rest_kernel(late_rows, second, first_ref, second_ref, pair_ref, whole_ref, ints_ref, part_ref, out_ref):
    step = pl.program_id(0)
    group_rows = out_ref.shape[0]
    size = group_rows // SEGMENTS
    per_first = second // size
    width = out_ref.shape[1] // COLUMNS
    for c in range(COLUMNS):
        cols = pl.ds(c * width, width)
        value = contract(ints_ref[...], whole_ref[cols, :])
        for s in range(SEGMENTS):
            low = s * size
            fst = first_ref[step * (group_rows // second) + s // per_first]
            snd = second_ref[pl.ds((s % per_first) * size, size), :]
            denom = (fst + snd) + pair_ref[:, cols]
            top = value[low:low + size] if low < late_rows else part_ref[pl.ds(low - late_rows, size), cols]
            out_ref[pl.ds(low, size), cols] = top * pl.reciprocal(denom)


def overlapped(nb, amplitudes, integrals, first_energy, second_energy, pair_energy):
    first_count, second_count, cd_count = integrals.shape
    rows, cols = amplitudes.shape
    pairs = rows * nb
    total = first_count * second_count
    group_rows = 4 * second_count
    groups = total // group_rows
    early = group_rows * EARLY // SEGMENTS
    late = group_rows - early
    grouped = integrals.reshape(groups, group_rows, cd_count)
    sends = 10 * nb
    whole, part = pl.pallas_call(
        functools.partial(gather_kernel, nb, early),
        out_shape=(
            jax.ShapeDtypeStruct((pairs, cd_count), amplitudes.dtype),
            jax.ShapeDtypeStruct((groups * early, pairs), jnp.float32),
        ),
        in_specs=[pl.BlockSpec(memory_space=pltpu.VMEM), pl.BlockSpec(memory_space=pl.ANY)],
        out_specs=(pl.BlockSpec(memory_space=pl.ANY), pl.BlockSpec(memory_space=pl.ANY)),
        scratch_shapes=[
            pltpu.VMEM((pairs, cd_count), amplitudes.dtype),
            pltpu.VMEM((4, groups, early, CORES * cols), integrals.dtype),
            pltpu.VMEM((nb, groups * early, rows), jnp.float32),
            pltpu.SemaphoreType.DMA((4 * CORES * nb,)),
            pltpu.SemaphoreType.DMA((sends,)),
            pltpu.SemaphoreType.DMA((1 + nb,)),
            pltpu.SemaphoreType.DMA((4,)),
            pltpu.SemaphoreType.DMA((nb,)),
        ],
        compiler_params=pltpu.CompilerParams(
            collective_id=0, has_side_effects=True, vmem_limit_bytes=60 * 2**20
        ),
        name="gather_and_start",
    )(amplitudes, grouped)
    out = pl.pallas_call(
        functools.partial(rest_kernel, late, second_count),
        grid=(groups,),
        out_shape=jax.ShapeDtypeStruct((total, pairs), jnp.float32),
        in_specs=[
            pl.BlockSpec(memory_space=pltpu.SMEM),
            pl.BlockSpec((second_count, 1), lambda i: (0, 0)),
            pl.BlockSpec((1, pairs), lambda i: (0, 0)),
            pl.BlockSpec((pairs, cd_count), lambda i: (0, 0), pipeline_mode=pl.Buffered(1)),
            pl.BlockSpec((None, late, cd_count), lambda i: (i, 0, 0)),
            pl.BlockSpec((early, pairs), lambda i: (i, 0)),
        ],
        out_specs=pl.BlockSpec((group_rows, pairs), lambda i: (i, 0)),
        compiler_params=pltpu.CompilerParams(vmem_limit_bytes=60 * 2**20),
        name="finish",
    )(first_energy, second_energy[:, None], pair_energy[None, :], whole, grouped, part)
    return out.reshape(first_count, second_count, pairs)


def on_device(na, nb, amplitudes, integrals, virt_energy, pair_energy):
    first_count, second_count, cd_count = integrals.shape
    first_energy = lax.dynamic_slice_in_dim(
        virt_energy, lax.axis_index("aa") * first_count, first_count, 0
    )
    second_energy = lax.dynamic_slice_in_dim(
        virt_energy, lax.axis_index("ba") * second_count, second_count, 0
    )
    rows, cols = amplitudes.shape
    fits = na == CORES * SIDE * SIDE and rows % 128 == 0 and cols % 128 == 0
    if fits and first_count % (4 * GROUP) == 0 and second_count % 128 == 0:
        return overlapped(nb, amplitudes, integrals, first_energy, second_energy, pair_energy)
    flat_ints = integrals.reshape(first_count * second_count, cd_count)
    all_rows = lax.all_gather(amplitudes, "ba", axis=0, tiled=True)
    whole = lax.all_gather(all_rows, "aa", axis=1, tiled=True)
    ladder = contract(flat_ints, whole).reshape(first_count, second_count, -1)
    denom = first_energy[:, None, None] + second_energy[None, :, None] + pair_energy[None, None, :]
    return ladder / denom


def solution(mesh):
    placed = (P("ba", "aa"), P("aa", "ba", None), P(), P())
    body = functools.partial(on_device, mesh.shape["aa"], mesh.shape["ba"])
    return jax.shard_map(
        body, mesh=mesh, in_specs=placed, out_specs=P("aa", "ba", None), check_vma=False
    )
```

time: 112 us -> 80.9 us (0.72)
  Pallas kernels: 0 us -> 77.4 us
  matrix products: 42 us -> 0 us
  waiting for transfers between devices: 35.6 us -> 0 us
  blocking collectives: 19.4 us -> 0 us
  between operations: 13.4 us -> 0.01 us
  local copies, waits for them, and re-layouts: 1.51 us -> 2.78 us
    pallas_call x0 -> x2, Pallas kernels: none -> 77.4 us  [the longest x1 42.1 us: overlapped(): pl.pallas_call(functools.partial(gather_kernel, nb, early), out_shape=(ja...]
    dot_general x1 -> x0, matrix products: 42 us -> none  [contract(): lax.dot_general(left, right, (((1,), (1,)), ((), ())), preferred_element_...]
    all_gather x1 -> x0, waiting for transfers between devices: 35.6 us -> none  [on_device(): whole = lax.all_gather(all_rows, 'aa', axis=1, tiled=True)]
    all_gather x1 -> x0, blocking collectives: 19.4 us -> none  [on_device(): all_rows = lax.all_gather(amplitudes, 'ba', axis=0, tiled=True)]
    broadcast_in_dim x0 -> x2, local copies, waits for them, and re-layouts: none -> 1.49 us  [overlapped(): second_energy[:, None]]
  transfers between devices with their start and end apart: 1 -> 0, of which waited for: 1 -> 0; matrix products, arithmetic and copies ran while one was open for 1% -> 0% of each run, Pallas kernels for 0% -> 0%
where the time goes in v1:
time: 80.9 us; the launch traced here: 80.2 us
  Pallas kernels  77.4 us (96%)
  local copies, waits for them, and re-layouts  2.78 us (3%)
    pallas_call x1, Pallas kernels, overlapped(): pl.pallas_call(functools.partial(gather_kernel, nb, early), out_shape=(ja...  42.1 us
    pallas_call x1, Pallas kernels, overlapped(): pl.pallas_call(functools.partial(rest_kernel, late, second_count), grid=(...  35.3 us

profile of v1, /device:TPU:0, one launch (start us, length us, event | category | flops | bytes accessed | tf_op | source)
XLA Modules:
  0.0 80.2 jit_solution(482215428655975342)
XLA Ops:
  0.0 0.8 dynamic-slice_bitcast_fusion
  0.8 1.3 %dynamic_slice.6.first_ref = f32[64]{0:T(128)} dynamic-slice(f32[512]{0:T(512)} %param.6, s32[]{:T(128)S(6)} %select_n.6), dynamic_slice_sizes={64} | dynamic-slice | bytes 516 | tf_op jit(solution)/shard_map/dynamic_slice | solution.py:268
  2.0 0.7 copy.5.second_ref
  2.8 42.1 %gather_and_start.1 = (bf16[1024,2048]{1,0:T(8,128)(2,1)}, f32[3072,1024]{1,0:T(8,128)}) custom-call(bf16[256,256]{1,0:T(8,128)(2,1)} %amp_ref.1, bf16[16,512,2048]{2,1,0:T(8,128)(2,1)} %bitcast.5), custom_call_target="tpu_custom_call" | custom-call | tf_op jit(solution)/shard_map/gather_and_start/pallas_call | solution.py:224
  44.9 35.3 %finish.1 = f32[8192,1024]{1,0:T(8,128)} custom-call(f32[64]{0:T(128)} %dynamic_slice.6.first_ref, f32[128,1]{1,0:T(8,128)} %copy.5.second_ref, f32[1,1024]{1,0:T(1,128)} %bitcast.7, bf16[1024,2048]{1,0:T(8,128)(2,1)} %get-tuple-element.7.whole_ref, bf16[16,512,2048]{2,1,0:T(8,128)(2,1)} %bitcast.6, f32[3072,1024]{1,0:T(8,128)} %get-tuple-element.8.part_ref), custom_call_target="tpu_custom_call" | custom-call | tf_op jit(solution)/shard_map/finish/pallas_call | solution.py:247
